TPU v7x, 32 devices: a whole 2x2x4 slice. The times are simulated.
32 devices in a mesh: row: 2 (over x), col: 4 (over y, core), rhs: 4 (over z).
Axes of the slice: x: 2, y: 2, z: 4, core: 2. Of those that a mesh axis runs over, the one named last changes fastest.
Arguments:
- right_side: float32 [2, 64, 8192], P('row', 'rhs', 'col'), may hold values from -6 to 6
- guess: float32 [2, 64, 8192], P('row', 'rhs', 'col'), may hold values from -6 to 6
- inverse: bfloat16 [2, 8192, 8192], P('row', 'rhs', 'col'), may hold values from -0.0625 to 0.0625
- left_factor: bfloat16 [2, 2, 64, 8192], P('row', None, None, 'col'), may hold values from -0.5 to 0.5
- right_factor: bfloat16 [2, 2, 64, 8192], P('row', None, None, 'col'), may hold values from -0.0625 to 0.0625
- ranks: int32 [2, 2], replicated, may hold values from 16 to 64
Outputs:
- solution: float32 [2, 64, 8192], P('row', 'rhs', 'col')
Inputs may be any that keep to these rules, and one draw needn't show every extreme that they name: ranks[i, j] is the rank of the block in block row i and block column j; diagonal entries are not read.
All inputs are finite; a program needn't handle non-finite values.
Results may differ from a plain program's by a relative error of at most 0.008.
Values may be sent and summed in bfloat16 or wider, within the bound.
A program may use at most 128 MiB of HBM per device.

v0:
```python
import jax
import jax.numpy as jnp
from jax import lax
from jax.sharding import PartitionSpec as P


def body(right_side, guess, inverse, left_factor, right_factor, ranks):
    blocks = lax.axis_size("row")
    mine = lax.axis_index("row")
    left = left_factor[0]
    right = right_factor[0]
    width = left.shape[1]
    keep = (lax.broadcasted_iota(jnp.int32, (blocks, blocks, width), 2) < ranks[:, :, None]).astype(
        jnp.float32
    )
    keep_mine = lax.dynamic_index_in_dim(keep, mine, 1, keepdims=False)
    partial_value = jnp.einsum(
        "rm,ikm->irk", guess[0].astype(jnp.bfloat16), right, preferred_element_type=jnp.float32
    )
    partial_value = partial_value * keep_mine[:, None, :]
    old_sum = lax.psum(partial_value, "col").astype(jnp.bfloat16)
    old_mine = lax.all_to_all(old_sum, "row", split_axis=0, concat_axis=0, tiled=True)
    later = lax.broadcasted_iota(jnp.int32, (blocks, 1, 1), 0) > mine
    old_kept = jnp.where(later, old_mine, jnp.zeros_like(old_mine))
    upper = jnp.einsum("jrk,jkm->rm", old_kept, left, preferred_element_type=jnp.float32)
    base = right_side[0] - upper
    lower = jnp.zeros_like(base)
    solution = jnp.zeros_like(base)
    for step in range(blocks):
        residue = (base - lower).astype(jnp.bfloat16)
        residue_full = lax.all_gather(residue, "col", axis=1, tiled=True)
        pieces = lax.all_to_all(residue_full, "rhs", split_axis=1, concat_axis=0, tiled=True)
        product = jnp.dot(pieces, inverse[0], preferred_element_type=jnp.float32)
        current = lax.psum_scatter(product, "rhs", scatter_dimension=0, tiled=True)
        solution = jnp.where(mine == step, current, solution)
        if step + 1 < blocks:
            coef = jnp.einsum(
                "rm,ikm->irk",
                current.astype(jnp.bfloat16),
                right,
                preferred_element_type=jnp.float32,
            )
            coef = coef * keep[:, step][:, None, :]
            coef = jnp.where(mine == step, coef, jnp.zeros_like(coef))
            shared = lax.psum(coef, ("row", "col")).astype(jnp.bfloat16)
            own_coef = lax.dynamic_index_in_dim(shared, mine, 0, keepdims=False)
            term = jnp.dot(own_coef, left[step], preferred_element_type=jnp.float32)
            lower = lower + jnp.where(mine > step, term, jnp.zeros_like(term))
    return solution[None]


def solution(mesh):
    in_specs = (
        P("row", "rhs", "col"),
        P("row", "rhs", "col"),
        P("row", "rhs", "col"),
        P("row", None, None, "col"),
        P("row", None, None, "col"),
        P(),
    )
    out_specs = P("row", "rhs", "col")
    return jax.shard_map(body, mesh=mesh, in_specs=in_specs, out_specs=out_specs, check_vma=False)
```

profile of v0, /device:TPU:0, one launch (start us, length us, event | category | flops | bytes accessed | tf_op | source)
XLA Modules:
  0.0 150.5 jit_solution(729392228866643291)
XLA Ops:
  6.5 0.0 copy-start
  6.5 0.8 copy.8
  7.4 0.1 compare_convert_fusion
  7.4 0.2 copy-done
  7.6 1.2 fusion.9
  8.8 12.7 %psum.14 = bf16[2,16,64]{2,1,0:T(8,128)(2,1)S(1)} all-reduce(f32[2,16,64]{2,1,0:T(8,128)S(1)} %fusion.9), channel_id=1, replica_groups=mesh['row'=2,'col'=4,'rhs'=4] {'col'}, use_global_device_ids=true, to_apply=%region_0.1 | all-reduce | flops 2048 | bytes 12288 | tf_op jit(solution)/shard_map/psum | solution.py:21
  21.5 0.7 reshape.18
  22.2 3.2 %all-to-all-start = ((bf16[2,2,512]{2,1,0:T(2,128)(2,1)}), bf16[2,2,512]{2,1,0:T(2,128)(2,1)S(1)}, u32[]{:S(2)}, u32[]{:S(2)}) async-start(bf16[2,2,512]{2,1,0:T(2,128)(2,1)} %reshape.18), calls=%async_computation | async-start | bytes 8192 | tf_op jit(solution)/shard_map/all_to_all | solution.py:22
  25.4 0.0 reduce-scatter.3.cloned.1.call-start
  25.5 3.7 %all-to-all-done = bf16[2,2,512]{2,1,0:T(2,128)(2,1)S(1)} async-done(((bf16[2,2,512]{2,1,0:T(2,128)(2,1)}), bf16[2,2,512]{2,1,0:T(2,128)(2,1)S(1)}, u32[]{:S(2)}, u32[]{:S(2)}) %all-to-all-start) | async-done | bytes 4128 | tf_op jit(solution)/shard_map/all_to_all | solution.py:22
  29.2 0.1 reshape.19
  29.3 1.4 fusion.26
  30.7 5.8 %all_gather.6 = bf16[16,8192]{1,0:T(8,128)(2,1)S(1)} all-gather(bf16[16,2048]{1,0:T(8,128)(2,1)S(1)} %get-tuple-element.7), channel_id=1, replica_groups=mesh['row'=2,'col'=4,'rhs'=4] {'col'}, dimensions={1}, use_global_device_ids=true | all-gather | bytes 327680 | tf_op jit(solution)/shard_map/all_gather | solution.py:31
  36.5 14.1 %all_to_all.43 = bf16[16,4,2048]{2,0,1:T(8,128)(2,1)S(1)} all-to-all(bf16[16,4,2048]{2,0,1:T(8,128)(2,1)S(1)} %bitcast.64), channel_id=1, replica_groups=mesh['row'=2,'col'=4,'rhs'=4] {'rhs'}, dimensions={1} | all-to-all | bytes 524288 | tf_op jit(solution)/shard_map/all_to_all | solution.py:32
  50.5 0.0 copy-start.1
  50.5 5.8 %fusion.2 = f32[64,2048]{1,0:T(8,128)} fusion(bf16[64,2048]{1,0:T(8,128)(2,1)S(1)} %bitcast.60, bf16[1,2048,2048]{2,1,0:T(8,128)(2,1)} %param.8), kind=kOutput, calls=%fused_computation.2 | convolution fusion | flops 536870912 | bytes 9175040 | tf_op jit(solution)/shard_map/dot_general | solution.py:33
  56.3 0.0 reduce-scatter.3.cloned.1.call-update
  56.4 0.0 reduce-scatter.5.cloned.1.call-start
  56.4 19.2 %reduce-scatter.3.cloned.1.call-done = f32[16,2048]{1,0:T(8,128)} async-done(((f32[64,2048]{1,0:T(8,128)}), f32[16,2048]{1,0:T(8,128)}) %reduce-scatter.3.cloned.1.call-update) | async-done | bytes 131088 | tf_op jit(solution)/shard_map/reduce_scatter | solution.py:34
  75.6 1.2 fusion.8
  76.8 22.3 %psum.15 = bf16[2,16,64]{2,1,0:T(8,128)(2,1)S(1)} all-reduce(f32[2,16,64]{2,1,0:T(8,128)S(1)} %fusion.8), channel_id=1, replica_groups=mesh['row'=2,'col'=4,'rhs'=4] {'row','col'}, use_global_device_ids=true, to_apply=%region_2.3 | all-reduce | flops 2048 | bytes 12288 | tf_op jit(solution)/shard_map/psum | solution.py:45
  99.2 0.0 copy-done.1
  99.2 0.2 fusion.6
  99.3 5.8 %all_gather.7 = bf16[16,8192]{1,0:T(8,128)(2,1)S(1)} all-gather(bf16[16,2048]{1,0:T(8,128)(2,1)S(1)} %fusion.6), channel_id=1, replica_groups=mesh['row'=2,'col'=4,'rhs'=4] {'col'}, dimensions={1}, use_global_device_ids=true | all-gather | bytes 327680 | tf_op jit(solution)/shard_map/all_gather | solution.py:31
  105.1 12.0 %all_to_all.44 = bf16[16,4,2048]{2,0,1:T(8,128)(2,1)S(1)} all-to-all(bf16[16,4,2048]{2,0,1:T(8,128)(2,1)S(1)} %bitcast.65), channel_id=1, replica_groups=mesh['row'=2,'col'=4,'rhs'=4] {'rhs'}, dimensions={1} | all-to-all | bytes 524288 | tf_op jit(solution)/shard_map/all_to_all | solution.py:32
  117.2 0.0 copy-start.2
  117.2 5.8 %fusion = f32[64,2048]{1,0:T(8,128)} fusion(bf16[64,2048]{1,0:T(8,128)(2,1)S(1)} %bitcast.61, bf16[1,2048,2048]{2,1,0:T(8,128)(2,1)} %param.8), kind=kOutput, calls=%fused_computation | convolution fusion | flops 536870912 | bytes 9175040 | tf_op jit(solution)/shard_map/dot_general | solution.py:33
  122.9 0.0 reduce-scatter.5.cloned.1.call-update
  123.0 20.0 %reduce-scatter.5.cloned.1.call-done = f32[16,2048]{1,0:T(8,128)} async-done(((f32[64,2048]{1,0:T(8,128)}), f32[16,2048]{1,0:T(8,128)}) %reduce-scatter.5.cloned.1.call-update) | async-done | bytes 131088 | tf_op jit(solution)/shard_map/reduce_scatter | solution.py:34
  143.0 0.0 copy-done.2
  143.0 0.7 select_bitcast_fusion
  (4 shorter events, 0.0 us)
Async XLA Ops:
  6.5 1.1 copy-start
  22.2 7.0 %all-to-all-start = ((bf16[2,2,512]{2,1,0:T(2,128)(2,1)}), bf16[2,2,512]{2,1,0:T(2,128)(2,1)S(1)}, u32[]{:S(2)}, u32[]{:S(2)}) async-start(bf16[2,2,512]{2,1,0:T(2,128)(2,1)} %reshape.18), calls=%async_computation | async-start | bytes 8192 | tf_op jit(solution)/shard_map/all_to_all | solution.py:22
  25.4 50.2 %reduce-scatter.3.cloned.1.call-start = ((), (), s32[]{:S(2)}) async-start(), calls=%async_computation.5 | async-start | bytes 655360 | tf_op jit(solution)/shard_map/reduce_scatter | solution.py:34
  50.5 48.6 %copy-start.1 = (bf16[1,2,64,2048]{3,2,1,0:T(8,128)(2,1)S(1)}, bf16[1,2,64,2048]{3,2,1,0:T(8,128)(2,1)}, u32[]{:S(2)}) copy-start(bf16[1,2,64,2048]{3,2,1,0:T(8,128)(2,1)} %param.9) | copy-start | bytes 1572868
  56.4 86.6 %reduce-scatter.5.cloned.1.call-start = ((), (), s32[]{:S(2)}) async-start(), calls=%async_computation.6 | async-start | bytes 655360 | tf_op jit(solution)/shard_map/reduce_scatter | solution.py:34
  117.2 25.8 %copy-start.2 = (f32[16,2048]{1,0:T(8,128)S(1)}, f32[16,2048]{1,0:T(8,128)}, u32[]{:S(2)}) copy-start(f32[16,2048]{1,0:T(8,128)} %reduce-scatter.3.cloned.1.call-done) | copy-start | bytes 393220
Sparse Core Ops, SparseCore 0:
  56.5 19.0 reduce-scatter.2
  123.1 19.8 reduce-scatter.4
where the time goes:
time: 151 us
  blocking collectives  72.7 us (48%)
  waiting for transfers between devices  43 us (28%)
  matrix products  15.5 us (10%)
  between operations  13.4 us (9%)
  starting transfers between devices  3.3 us (2%)
  local copies, waits for them, and re-layouts  1.79 us (1%)
    reduce_scatter x2, waiting for transfers between devices, body(): current = lax.psum_scatter(product, 'rhs', scatter_dimension=0, tiled=True)  39.2 us
    all_to_all x2, blocking collectives, body(): lax.all_to_all(residue_full, 'rhs', split_axis=1, concat_axis=0, tiled=True)  26.1 us
    psum x1, blocking collectives, body(): shared = lax.psum(coef, ('row', 'col')).astype(jnp.bfloat16)  22.3 us
    psum x1, blocking collectives, body(): old_sum = lax.psum(partial_value, 'col').astype(jnp.bfloat16)  12.7 us
    dot_general x2, matrix products, body(): product = jnp.dot(pieces, inverse[0], preferred_element_type=jnp.float32)  11.6 us
    all_gather x2, blocking collectives, body(): residue_full = lax.all_gather(residue, 'col', axis=1, tiled=True)  11.6 us
    all_to_all x1, waiting for transfers between devices, body(): lax.all_to_all(old_sum, 'row', split_axis=0, concat_axis=0, tiled=True)  3.71 us
    all_to_all x1, starting transfers between devices, body(): lax.all_to_all(old_sum, 'row', split_axis=0, concat_axis=0, tiled=True)  3.22 us
  transfers between devices with their start and end apart: 3, of which 3 were waited for; matrix products, arithmetic and copies ran while one was open for 0% of the time, Pallas kernels for 0%

commit v1 on v0

--- a/solution.py
+++ b/solution.py
@@ -18,7 +18,7 @@
         "rm,ikm->irk", guess[0].astype(jnp.bfloat16), right, preferred_element_type=jnp.float32
     )
     partial_value = partial_value * keep_mine[:, None, :]
-    old_sum = lax.psum(partial_value, "col").astype(jnp.bfloat16)
+    old_sum = jnp.sum(lax.all_gather(partial_value, "col"), axis=0).astype(jnp.bfloat16)
     old_mine = lax.all_to_all(old_sum, "row", split_axis=0, concat_axis=0, tiled=True)
     later = lax.broadcasted_iota(jnp.int32, (blocks, 1, 1), 0) > mine
     old_kept = jnp.where(later, old_mine, jnp.zeros_like(old_mine))

time: 151 us -> 146 us (0.967)
  blocking collectives: 72.7 us -> 66.7 us
    psum x1 -> x0, blocking collectives: 12.7 us -> none  [body(): old_sum = lax.psum(partial_value, 'col').astype(jnp.bfloat16)]
    all_gather x0 -> x1, blocking collectives: none -> 6.22 us  [body(): lax.all_gather(partial_value, 'col')]
where the time goes in v1:
time: 146 us; the launch traced here: 145 us
  blocking collectives  66.7 us (46%)
  waiting for transfers between devices  43.9 us (30%)
  matrix products  15.5 us (11%)
  between operations  13.4 us (9%)
  starting transfers between devices  3.31 us (2%)
  local copies, waits for them, and re-layouts  1.79 us (1%)
    reduce_scatter x2, waiting for transfers between devices, body(): current = lax.psum_scatter(product, 'rhs', scatter_dimension=0, tiled=True)  40.1 us
    all_to_all x2, blocking collectives, body(): lax.all_to_all(residue_full, 'rhs', split_axis=1, concat_axis=0, tiled=True)  26.1 us
    psum x1, blocking collectives, body(): shared = lax.psum(coef, ('row', 'col')).astype(jnp.bfloat16)  22.4 us
    all_gather x2, blocking collectives, body(): residue_full = lax.all_gather(residue, 'col', axis=1, tiled=True)  12 us
    dot_general x2, matrix products, body(): product = jnp.dot(pieces, inverse[0], preferred_element_type=jnp.float32)  11.6 us
    all_gather x1, blocking collectives, body(): lax.all_gather(partial_value, 'col')  6.22 us
    all_to_all x1, waiting for transfers between devices, body(): lax.all_to_all(old_sum, 'row', split_axis=0, concat_axis=0, tiled=True)  3.76 us
    all_to_all x1, starting transfers between devices, body(): lax.all_to_all(old_sum, 'row', split_axis=0, concat_axis=0, tiled=True)  3.25 us
  transfers between devices with their start and end apart: 3, of which 3 were waited for; matrix products, arithmetic and copies ran while one was open for 0% of the time, Pallas kernels for 0%

profile of v1, /device:TPU:0, one launch (start us, length us, event | category | flops | bytes accessed | tf_op | source)
XLA Modules:
  0.0 145.5 jit_solution(7429441154396665633)
XLA Ops:
  6.5 0.0 copy-start
  6.5 0.8 copy.11
  7.4 0.1 compare_convert_fusion
  7.4 0.2 copy-done
  7.6 1.2 fusion.9
  8.8 6.2 %all-gather = f32[8,16,64]{2,1,0:T(8,128)S(1)} all-gather(f32[2,16,64]{2,1,0:T(8,128)S(1)} %fusion.9), channel_id=2, replica_groups=mesh['row'=2,'col'=4,'rhs'=4] {'col'}, dimensions={0}, use_global_device_ids=true | all-gather | bytes 40960 | tf_op jit(solution)/shard_map/all_gather | solution.py:21
  15.0 0.7 reshape.19
  15.7 3.3 %all-to-all-start = ((bf16[2,2,512]{2,1,0:T(2,128)(2,1)}), bf16[2,2,512]{2,1,0:T(2,128)(2,1)S(1)}, u32[]{:S(2)}, u32[]{:S(2)}) async-start(bf16[2,2,512]{2,1,0:T(2,128)(2,1)} %reshape.19), calls=%async_computation | async-start | bytes 8192 | tf_op jit(solution)/shard_map/all_to_all | solution.py:22
  19.0 0.0 reduce-scatter.3.cloned.1.call-start
  19.0 3.8 %all-to-all-done = bf16[2,2,512]{2,1,0:T(2,128)(2,1)S(1)} async-done(((bf16[2,2,512]{2,1,0:T(2,128)(2,1)}), bf16[2,2,512]{2,1,0:T(2,128)(2,1)S(1)}, u32[]{:S(2)}, u32[]{:S(2)}) %all-to-all-start) | async-done | bytes 4128 | tf_op jit(solution)/shard_map/all_to_all | solution.py:22
  22.8 0.1 reshape.20
  22.8 1.4 fusion.26
  24.2 6.2 %all_gather.14 = bf16[16,8192]{1,0:T(8,128)(2,1)S(1)} all-gather(bf16[16,2048]{1,0:T(8,128)(2,1)S(1)} %get-tuple-element.7), channel_id=1, replica_groups=mesh['row'=2,'col'=4,'rhs'=4] {'col'}, dimensions={1}, use_global_device_ids=true | all-gather | bytes 327680 | tf_op jit(solution)/shard_map/all_gather | solution.py:31
  30.5 14.1 %all_to_all.43 = bf16[16,4,2048]{2,0,1:T(8,128)(2,1)S(1)} all-to-all(bf16[16,4,2048]{2,0,1:T(8,128)(2,1)S(1)} %bitcast.65), channel_id=1, replica_groups=mesh['row'=2,'col'=4,'rhs'=4] {'rhs'}, dimensions={1} | all-to-all | bytes 524288 | tf_op jit(solution)/shard_map/all_to_all | solution.py:32
  44.5 0.0 copy-start.1
  44.5 5.8 %fusion.2 = f32[64,2048]{1,0:T(8,128)} fusion(bf16[64,2048]{1,0:T(8,128)(2,1)S(1)} %bitcast.61, bf16[1,2048,2048]{2,1,0:T(8,128)(2,1)} %param.8), kind=kOutput, calls=%fused_computation.2 | convolution fusion | flops 536870912 | bytes 9175040 | tf_op jit(solution)/shard_map/dot_general | solution.py:33
  50.3 0.0 reduce-scatter.3.cloned.1.call-update
  50.3 0.0 reduce-scatter.5.cloned.1.call-start
  50.4 20.1 %reduce-scatter.3.cloned.1.call-done = f32[16,2048]{1,0:T(8,128)} async-done(((f32[64,2048]{1,0:T(8,128)}), f32[16,2048]{1,0:T(8,128)}) %reduce-scatter.3.cloned.1.call-update) | async-done | bytes 131088 | tf_op jit(solution)/shard_map/reduce_scatter | solution.py:34
  70.5 1.2 fusion.8
  71.7 22.4 %psum.7 = bf16[2,16,64]{2,1,0:T(8,128)(2,1)S(1)} all-reduce(f32[2,16,64]{2,1,0:T(8,128)S(1)} %fusion.8), channel_id=1, replica_groups=mesh['row'=2,'col'=4,'rhs'=4] {'row','col'}, use_global_device_ids=true, to_apply=%region_2.3 | all-reduce | flops 2048 | bytes 12288 | tf_op jit(solution)/shard_map/psum | solution.py:45
  94.1 0.0 copy-done.1
  94.1 0.2 fusion.6
  94.3 5.8 %all_gather.15 = bf16[16,8192]{1,0:T(8,128)(2,1)S(1)} all-gather(bf16[16,2048]{1,0:T(8,128)(2,1)S(1)} %fusion.6), channel_id=1, replica_groups=mesh['row'=2,'col'=4,'rhs'=4] {'col'}, dimensions={1}, use_global_device_ids=true | all-gather | bytes 327680 | tf_op jit(solution)/shard_map/all_gather | solution.py:31
  100.1 12.0 %all_to_all.44 = bf16[16,4,2048]{2,0,1:T(8,128)(2,1)S(1)} all-to-all(bf16[16,4,2048]{2,0,1:T(8,128)(2,1)S(1)} %bitcast.66), channel_id=1, replica_groups=mesh['row'=2,'col'=4,'rhs'=4] {'rhs'}, dimensions={1} | all-to-all | bytes 524288 | tf_op jit(solution)/shard_map/all_to_all | solution.py:32
  112.1 0.0 copy-start.2
  112.1 5.8 %fusion = f32[64,2048]{1,0:T(8,128)} fusion(bf16[64,2048]{1,0:T(8,128)(2,1)S(1)} %bitcast.62, bf16[1,2048,2048]{2,1,0:T(8,128)(2,1)} %param.8), kind=kOutput, calls=%fused_computation | convolution fusion | flops 536870912 | bytes 9175040 | tf_op jit(solution)/shard_map/dot_general | solution.py:33
  117.9 0.0 reduce-scatter.5.cloned.1.call-update
  117.9 20.0 %reduce-scatter.5.cloned.1.call-done = f32[16,2048]{1,0:T(8,128)} async-done(((f32[64,2048]{1,0:T(8,128)}), f32[16,2048]{1,0:T(8,128)}) %reduce-scatter.5.cloned.1.call-update) | async-done | bytes 131088 | tf_op jit(solution)/shard_map/reduce_scatter | solution.py:34
  137.9 0.0 copy-done.2
  137.9 0.7 select_bitcast_fusion
  (5 shorter events, 0.1 us)
Async XLA Ops:
  6.5 1.1 copy-start
  15.7 7.0 %all-to-all-start = ((bf16[2,2,512]{2,1,0:T(2,128)(2,1)}), bf16[2,2,512]{2,1,0:T(2,128)(2,1)S(1)}, u32[]{:S(2)}, u32[]{:S(2)}) async-start(bf16[2,2,512]{2,1,0:T(2,128)(2,1)} %reshape.19), calls=%async_computation | async-start | bytes 8192 | tf_op jit(solution)/shard_map/all_to_all | solution.py:22
  19.0 51.6 %reduce-scatter.3.cloned.1.call-start = ((), (), s32[]{:S(2)}) async-start(), calls=%async_computation.5 | async-start | bytes 655360 | tf_op jit(solution)/shard_map/reduce_scatter | solution.py:34
  44.5 49.6 %copy-start.1 = (bf16[1,2,64,2048]{3,2,1,0:T(8,128)(2,1)S(1)}, bf16[1,2,64,2048]{3,2,1,0:T(8,128)(2,1)}, u32[]{:S(2)}) copy-start(bf16[1,2,64,2048]{3,2,1,0:T(8,128)(2,1)} %param.9) | copy-start | bytes 1572868
  50.3 87.6 %reduce-scatter.5.cloned.1.call-start = ((), (), s32[]{:S(2)}) async-start(), calls=%async_computation.6 | async-start | bytes 655360 | tf_op jit(solution)/shard_map/reduce_scatter | solution.py:34
  112.1 25.8 %copy-start.2 = (f32[16,2048]{1,0:T(8,128)S(1)}, f32[16,2048]{1,0:T(8,128)}, u32[]{:S(2)}) copy-start(f32[16,2048]{1,0:T(8,128)} %reduce-scatter.3.cloned.1.call-done) | copy-start | bytes 393220
Sparse Core Ops, SparseCore 0:
  50.5 20.0 reduce-scatter.2
  118.0 19.8 reduce-scatter.4

commit v2 on v0

--- a/solution.py
+++ b/solution.py
@@ -28,7 +28,7 @@
     solution = jnp.zeros_like(base)
     for step in range(blocks):
         residue = (base - lower).astype(jnp.bfloat16)
-        residue_full = lax.all_gather(residue, "col", axis=1, tiled=True)
+        residue_full = jnp.concatenate(lax.all_gather(residue, "col"), axis=1)
         pieces = lax.all_to_all(residue_full, "rhs", split_axis=1, concat_axis=0, tiled=True)
         product = jnp.dot(pieces, inverse[0], preferred_element_type=jnp.float32)
         current = lax.psum_scatter(product, "rhs", scatter_dimension=0, tiled=True)

time: 151 us -> 151 us (level)
  no operation moved by 1% of the time
where the time goes in v2:
time: 151 us; the launch traced here: 150 us
  blocking collectives  72.7 us (48%)
  waiting for transfers between devices  43 us (28%)
  matrix products  15.5 us (10%)
  between operations  13.4 us (9%)
  starting transfers between devices  3.3 us (2%)
  local copies, waits for them, and re-layouts  1.76 us (1%)
    reduce_scatter x2, waiting for transfers between devices, body(): current = lax.psum_scatter(product, 'rhs', scatter_dimension=0, tiled=True)  39.2 us
    all_to_all x2, blocking collectives, body(): lax.all_to_all(residue_full, 'rhs', split_axis=1, concat_axis=0, tiled=True)  26.1 us
    psum x1, blocking collectives, body(): shared = lax.psum(coef, ('row', 'col')).astype(jnp.bfloat16)  22.3 us
    psum x1, blocking collectives, body(): old_sum = lax.psum(partial_value, 'col').astype(jnp.bfloat16)  12.7 us
    dot_general x2, matrix products, body(): product = jnp.dot(pieces, inverse[0], preferred_element_type=jnp.float32)  11.6 us
    all_gather x2, blocking collectives, body(): residue_full = jnp.concatenate(lax.all_gather(residue, 'col'), axis=1)  11.6 us
    all_to_all x1, waiting for transfers between devices, body(): lax.all_to_all(old_sum, 'row', split_axis=0, concat_axis=0, tiled=True)  3.71 us
    all_to_all x1, starting transfers between devices, body(): lax.all_to_all(old_sum, 'row', split_axis=0, concat_axis=0, tiled=True)  3.22 us
  transfers between devices with their start and end apart: 3, of which 3 were waited for; matrix products, arithmetic and copies ran while one was open for 0% of the time, Pallas kernels for 0%

profile of v2, /device:TPU:0, one launch (start us, length us, event | category | flops | bytes accessed | tf_op | source)
XLA Modules:
  0.0 150.4 jit_solution(9258570014789062642)
XLA Ops:
  6.5 0.0 copy-start
  6.5 0.8 copy.7
  7.4 0.1 compare_convert_fusion
  7.4 0.2 copy-done
  7.6 1.2 fusion.9
  8.8 12.7 %psum.14 = bf16[2,16,64]{2,1,0:T(8,128)(2,1)S(1)} all-reduce(f32[2,16,64]{2,1,0:T(8,128)S(1)} %fusion.9), channel_id=1, replica_groups=mesh['row'=2,'col'=4,'rhs'=4] {'col'}, use_global_device_ids=true, to_apply=%region_0.1 | all-reduce | flops 2048 | bytes 12288 | tf_op jit(solution)/shard_map/psum | solution.py:21
  21.5 0.7 reshape.32
  22.2 3.2 %all-to-all-start = ((bf16[2,2,512]{2,1,0:T(2,128)(2,1)}), bf16[2,2,512]{2,1,0:T(2,128)(2,1)S(1)}, u32[]{:S(2)}, u32[]{:S(2)}) async-start(bf16[2,2,512]{2,1,0:T(2,128)(2,1)} %reshape.32), calls=%async_computation | async-start | bytes 8192 | tf_op jit(solution)/shard_map/all_to_all | solution.py:22
  25.4 0.0 reduce-scatter.3.cloned.1.call-start
  25.5 3.7 %all-to-all-done = bf16[2,2,512]{2,1,0:T(2,128)(2,1)S(1)} async-done(((bf16[2,2,512]{2,1,0:T(2,128)(2,1)}), bf16[2,2,512]{2,1,0:T(2,128)(2,1)S(1)}, u32[]{:S(2)}, u32[]{:S(2)}) %all-to-all-start) | async-done | bytes 4128 | tf_op jit(solution)/shard_map/all_to_all | solution.py:22
  29.2 0.1 reshape.33
  29.3 1.4 fusion.26
  30.7 5.8 %all-gather = bf16[64,2048]{1,0:T(8,128)(2,1)S(1)} all-gather(bf16[16,2048]{1,0:T(8,128)(2,1)S(1)} %get-tuple-element.7), channel_id=2, replica_groups=mesh['row'=2,'col'=4,'rhs'=4] {'col'}, dimensions={0}, use_global_device_ids=true | all-gather | bytes 327680 | tf_op jit(solution)/shard_map/all_gather | solution.py:31
  36.5 14.0 %all_to_all.37 = bf16[16,4,2048]{2,0,1:T(8,128)(2,1)S(1)} all-to-all(bf16[16,4,2048]{2,0,1:T(8,128)(2,1)S(1)} %bitcast.60), channel_id=1, replica_groups=mesh['row'=2,'col'=4,'rhs'=4] {'rhs'}, dimensions={1} | all-to-all | bytes 524288 | tf_op jit(solution)/shard_map/all_to_all | solution.py:32
  50.5 0.0 copy-start.1
  50.5 5.8 %fusion.2 = f32[64,2048]{1,0:T(8,128)} fusion(bf16[64,2048]{1,0:T(8,128)(2,1)S(1)} %bitcast.58, bf16[1,2048,2048]{2,1,0:T(8,128)(2,1)} %param.8), kind=kOutput, calls=%fused_computation.2 | convolution fusion | flops 536870912 | bytes 9175040 | tf_op jit(solution)/shard_map/dot_general | solution.py:33
  56.3 0.0 reduce-scatter.3.cloned.1.call-update
  56.3 0.0 reduce-scatter.5.cloned.1.call-start
  56.4 19.2 %reduce-scatter.3.cloned.1.call-done = f32[16,2048]{1,0:T(8,128)} async-done(((f32[64,2048]{1,0:T(8,128)}), f32[16,2048]{1,0:T(8,128)}) %reduce-scatter.3.cloned.1.call-update) | async-done | bytes 131088 | tf_op jit(solution)/shard_map/reduce_scatter | solution.py:34
  75.6 1.2 fusion.8
  76.8 22.3 %psum.15 = bf16[2,16,64]{2,1,0:T(8,128)(2,1)S(1)} all-reduce(f32[2,16,64]{2,1,0:T(8,128)S(1)} %fusion.8), channel_id=1, replica_groups=mesh['row'=2,'col'=4,'rhs'=4] {'row','col'}, use_global_device_ids=true, to_apply=%region_2.3 | all-reduce | flops 2048 | bytes 12288 | tf_op jit(solution)/shard_map/psum | solution.py:45
  99.1 0.0 copy-done.1
  99.1 0.2 fusion.6
  99.3 5.8 %all-gather.1 = bf16[64,2048]{1,0:T(8,128)(2,1)S(1)} all-gather(bf16[16,2048]{1,0:T(8,128)(2,1)S(1)} %fusion.6), channel_id=3, replica_groups=mesh['row'=2,'col'=4,'rhs'=4] {'col'}, dimensions={0}, use_global_device_ids=true | all-gather | bytes 327680 | tf_op jit(solution)/shard_map/all_gather | solution.py:31
  105.1 12.0 %all_to_all.38 = bf16[16,4,2048]{2,0,1:T(8,128)(2,1)S(1)} all-to-all(bf16[16,4,2048]{2,0,1:T(8,128)(2,1)S(1)} %bitcast.61), channel_id=1, replica_groups=mesh['row'=2,'col'=4,'rhs'=4] {'rhs'}, dimensions={1} | all-to-all | bytes 524288 | tf_op jit(solution)/shard_map/all_to_all | solution.py:32
  117.1 0.0 copy-start.2
  117.1 5.8 %fusion = f32[64,2048]{1,0:T(8,128)} fusion(bf16[64,2048]{1,0:T(8,128)(2,1)S(1)} %bitcast.59, bf16[1,2048,2048]{2,1,0:T(8,128)(2,1)} %param.8), kind=kOutput, calls=%fused_computation | convolution fusion | flops 536870912 | bytes 9175040 | tf_op jit(solution)/shard_map/dot_general | solution.py:33
  122.9 0.0 reduce-scatter.5.cloned.1.call-update
  122.9 20.0 %reduce-scatter.5.cloned.1.call-done = f32[16,2048]{1,0:T(8,128)} async-done(((f32[64,2048]{1,0:T(8,128)}), f32[16,2048]{1,0:T(8,128)}) %reduce-scatter.5.cloned.1.call-update) | async-done | bytes 131088 | tf_op jit(solution)/shard_map/reduce_scatter | solution.py:34
  142.9 0.0 copy-done.2
  142.9 0.7 select_bitcast_fusion
  (2 shorter events, 0.0 us)
Async XLA Ops:
  6.5 1.1 copy-start
  22.2 7.0 %all-to-all-start = ((bf16[2,2,512]{2,1,0:T(2,128)(2,1)}), bf16[2,2,512]{2,1,0:T(2,128)(2,1)S(1)}, u32[]{:S(2)}, u32[]{:S(2)}) async-start(bf16[2,2,512]{2,1,0:T(2,128)(2,1)} %reshape.32), calls=%async_computation | async-start | bytes 8192 | tf_op jit(solution)/shard_map/all_to_all | solution.py:22
  25.4 50.1 %reduce-scatter.3.cloned.1.call-start = ((), (), s32[]{:S(2)}) async-start(), calls=%async_computation.5 | async-start | bytes 655360 | tf_op jit(solution)/shard_map/reduce_scatter | solution.py:34
  50.5 48.6 %copy-start.1 = (bf16[1,2,64,2048]{3,2,1,0:T(8,128)(2,1)S(1)}, bf16[1,2,64,2048]{3,2,1,0:T(8,128)(2,1)}, u32[]{:S(2)}) copy-start(bf16[1,2,64,2048]{3,2,1,0:T(8,128)(2,1)} %param.9) | copy-start | bytes 1572868
  56.3 86.6 %reduce-scatter.5.cloned.1.call-start = ((), (), s32[]{:S(2)}) async-start(), calls=%async_computation.6 | async-start | bytes 655360 | tf_op jit(solution)/shard_map/reduce_scatter | solution.py:34
  117.1 25.8 %copy-start.2 = (f32[16,2048]{1,0:T(8,128)S(1)}, f32[16,2048]{1,0:T(8,128)}, u32[]{:S(2)}) copy-start(f32[16,2048]{1,0:T(8,128)} %reduce-scatter.3.cloned.1.call-done) | copy-start | bytes 393220
Sparse Core Ops, SparseCore 0:
  56.4 19.0 reduce-scatter.2
  123.0 19.8 reduce-scatter.4
